TPU v7x, 128 devices: a whole 4x4x4 slice. The times are simulated.
128 devices in a mesh: space: 16 (over x, z), mem: 8 (over y, core).
Axes of the slice: x: 4, y: 4, z: 4, core: 2. Of those that a mesh axis runs over, the one named last changes fastest.
Arguments:
- ensemble_state: bfloat16 [256, 1024, 256], P('mem', 'space'), may hold values from -6 to 6
- obs_ens: bfloat16 [256, 1024, 128], P('mem', 'space'), may hold values from -6 to 6
- innovation: float32 [1024, 128], P('space'), may hold values from -6 to 6
- obs_prec: float32 [1024, 128], P('space'), may hold values from 0.25 to 2
- block_list: int32 [1024, 8], P('space'), may hold values from 0 to 1023, as said below
- block_count: int32 [1024], P('space'), may hold values from 1 to 8
- loc_weight: float32 [1024, 8], P('space'), may hold values from 0.1 to 1
- prior_weight: float32 [1024, 256], P('space'), may hold values from 0.1 to 10, as said below
Outputs:
- analysis: bfloat16 [256, 1024, 256], P('mem', 'space')
Inputs may be any that keep to these rules, and one draw needn't show every extreme that they name: `block_list`: among the 64 entries of the regions r with the same r // 8, at most 6 name blocks b with the same b // 64, and exactly 6 do for one such value. `prior_weight`: Positive.
All inputs are finite; a program needn't handle non-finite values.
Results may differ from a plain program's by a relative error of at most 0.012.
Values may be sent and summed in bfloat16 or wider, within the bound.
A program may use at most 128 MiB of HBM per device.

v0:
```python
import jax
import jax.numpy as jnp
from jax import lax
from jax.sharding import PartitionSpec as P

INFLATION = 1.1


def transform(gram_blocks, projection, prior_rows):
    highest = lax.Precision.HIGHEST
    members = gram_blocks.shape[-1]
    shares = prior_rows / jnp.sum(prior_rows, axis=1, keepdims=True)
    root_q = jnp.sqrt(members * shares)
    left_term = jnp.einsum("rk,rkj->rj", shares, gram_blocks, precision=highest)
    centred = gram_blocks - left_term[:, None, :]
    right_term = jnp.einsum("rik,rk->ri", centred, shares, precision=highest)
    centred = centred - right_term[:, :, None]
    identity = jnp.eye(members, dtype=jnp.float32)
    system = (
        root_q[:, :, None] * centred * root_q[:, None, :] + (members - 1) / INFLATION * identity
    )
    vector = root_q * (projection - jnp.sum(shares * projection, axis=1, keepdims=True))
    factor = jnp.linalg.cholesky(system)
    inverse = jax.scipy.linalg.solve_triangular(
        factor, jnp.broadcast_to(identity, system.shape), lower=True
    )
    solved = jnp.einsum("rij,rj->ri", inverse, vector, precision=highest)
    weights = jnp.einsum("rji,rj->ri", inverse, solved, precision=highest)
    spread = jnp.sqrt(members - 1.0) * jnp.transpose(inverse, (0, 2, 1))
    mixing = root_q[:, :, None] * (weights[:, :, None] + spread)
    mixing = (
        mixing - shares[:, :, None] * jnp.sum(mixing, axis=1, keepdims=True) + shares[:, :, None]
    )
    return mixing


def body(
    ensemble_state, obs_ens, innovation, obs_prec, block_list, block_count, loc_weight, prior_weight
):
    spaces = lax.axis_size("space")
    mem_count = lax.axis_size("mem")
    members_dev = ensemble_state.shape[0]
    members = members_dev * mem_count
    regions_dev = ensemble_state.shape[1]
    group_size = regions_dev // mem_count
    blocks_dev = obs_ens.shape[1]
    obs_width = obs_ens.shape[2]
    slot_count = block_list.shape[1]
    entries = group_size * slot_count
    capacity = 3 * entries // (2 * spaces)
    mem_index = lax.axis_index("mem")
    first_row = mem_index * group_size
    block_ids = lax.dynamic_slice_in_dim(block_list, first_row, group_size, 0).reshape(entries)
    counts = lax.dynamic_slice_in_dim(block_count, first_row, group_size, 0)
    loc_rows = lax.dynamic_slice_in_dim(loc_weight, first_row, group_size, 0)
    prior_rows = lax.dynamic_slice_in_dim(prior_weight, first_row, group_size, 0)
    target = block_ids // blocks_dev
    local_ids = block_ids % blocks_dev
    onehot = (target[:, None] == jnp.arange(spaces, dtype=jnp.int32)[None, :]).astype(jnp.int32)
    slot_rank = jnp.sum(onehot * jnp.cumsum(onehot, axis=0), axis=1) - 1
    request_table = jnp.zeros((spaces, capacity), jnp.int32).at[target, slot_rank].set(local_ids)
    wanted = jnp.broadcast_to(request_table[:, None, :], (spaces, mem_count, capacity))
    wanted = wanted.reshape(spaces * mem_count, capacity)
    asked_ids = lax.all_to_all(wanted, ("space", "mem"), split_axis=0, concat_axis=0, tiled=True)
    outgoing = jnp.take(obs_ens, asked_ids, axis=1)
    arrived = lax.all_to_all(outgoing, ("space", "mem"), split_axis=1, concat_axis=1, tiled=True)
    arrived = arrived.reshape(members_dev, spaces, mem_count, capacity, obs_width)
    picked = arrived[:, target, :, slot_rank, :]
    picked = jnp.transpose(picked, (2, 1, 0, 3)).reshape(members, entries, obs_width)
    asked_grid = asked_ids.reshape(spaces, mem_count, capacity)
    from_peers = lax.dynamic_index_in_dim(asked_grid, mem_index, axis=1, keepdims=False)
    error_prec = jnp.take(obs_prec, from_peers, axis=0)
    error_innov = jnp.take(innovation, from_peers, axis=0)
    got_prec, got_innov = (
        lax.all_to_all(error_prec, "space", split_axis=0, concat_axis=0, tiled=True),
        lax.all_to_all(error_innov, "space", split_axis=0, concat_axis=0, tiled=True),
    )
    prec_rows = got_prec[target, slot_rank]
    innov_rows = got_innov[target, slot_rank]
    active = (jnp.arange(slot_count, dtype=jnp.int32)[None, :] < counts[:, None]).astype(
        jnp.float32
    )
    obs_weight = (active * loc_rows).reshape(entries)[:, None] * prec_rows
    obs_scale = jnp.sqrt(obs_weight)
    scaled = (picked.astype(jnp.float32) * obs_scale[None]).astype(jnp.bfloat16)
    shaped = scaled.reshape(members, group_size, slot_count, obs_width)
    gram_blocks = jnp.einsum("krlo,jrlo->rkj", shaped, shaped, preferred_element_type=jnp.float32)
    weighted_innov = (obs_scale * innov_rows).reshape(group_size, slot_count, obs_width)
    projection = jnp.einsum(
        "krlo,rlo->rk", shaped, weighted_innov, preferred_element_type=jnp.float32
    )
    mixing = transform(gram_blocks, projection, prior_rows)
    mix_high = mixing.astype(jnp.bfloat16)
    mix_low = (mixing - mix_high.astype(jnp.float32)).astype(jnp.bfloat16)
    mix_parts = jnp.concatenate([mix_high, mix_low], axis=2)
    region_states = lax.all_to_all(ensemble_state, "mem", split_axis=1, concat_axis=0, tiled=True)
    both_parts = jnp.einsum(
        "krp,rkj->jrp", region_states, mix_parts, preferred_element_type=jnp.float32
    )
    updated = (both_parts[:members] + both_parts[members:]).astype(jnp.bfloat16)
    return lax.all_to_all(updated, "mem", split_axis=0, concat_axis=1, tiled=True)


def solution(mesh):
    return jax.shard_map(
        body,
        mesh=mesh,
        in_specs=(
            P("mem", "space", None),
            P("mem", "space", None),
            P("space", None),
            P("space", None),
            P("space", None),
            P("space"),
            P("space", None),
            P("space", None),
        ),
        out_specs=P("mem", "space", None),
        check_vma=False,
    )
```

profile of v0, /device:TPU:1, one launch (start us, length us, event | category | flops | bytes accessed | tf_op | source)
XLA Modules:
  0.0 712.9 jit_solution(11391945641153206880)
XLA Ops:
  0.0 0.9 constant_dynamic-slice_fusion.2
  1.3 0.2 select_reduce_fusion.2
  1.6 3.5 scatter_fusion
  5.1 0.6 broadcast_in_dim.30.clone
  5.8 11.5 %all-to-all-start = ((s32[128,1,6]{2,1,0:T(1,128)}), s32[128,1,6]{2,1,0:T(1,128)S(1)}, u32[]{:S(2)}, u32[]{:S(2)}) async-start(s32[128,1,6]{2,1,0:T(1,128)} %bitcast.3), calls=%async_computation | async-start | bytes 131072 | tf_op jit(solution)/shard_map/all_to_all | solution.py:64
  17.3 9.4 %all-to-all-done = s32[128,1,6]{2,1,0:T(1,128)S(1)} async-done(((s32[128,1,6]{2,1,0:T(1,128)}), s32[128,1,6]{2,1,0:T(1,128)S(1)}, u32[]{:S(2)}, u32[]{:S(2)}) %all-to-all-start) | async-done | bytes 3104 | tf_op jit(solution)/shard_map/all_to_all | solution.py:64
  27.0 1.4 gather_fusion.4
  28.4 0.6 gather_fusion.5
  29.1 0.7 broadcast_select_fusion.1
  29.8 9.7 %all_to_all.66 = f32[16,6,128]{2,1,0:T(8,128)S(1)} all-to-all(f32[16,6,128]{2,1,0:T(8,128)S(1)} %get-tuple-element.39), channel_id=1, replica_groups=mesh['space'=16,'mem'=8] {'space'}, dimensions={0} | all-to-all | bytes 98304 | tf_op jit(solution)/shard_map/all_to_all | solution.py:75
  39.6 3.5 all-to-all-start.3
  43.1 1.6 copy.140
  44.6 4.9 all-to-all-done.3
  49.5 6.6 all-to-all-start.4
  56.3 29.1 %gather_fusion = bf16[768,32,128]{2,0,1:T(8,128)(2,1)} fusion(bf16[32,64,128]{2,1,0:T(8,128)(2,1)S(1)} %copy-done, s32[1024]{0:T(1024)S(1)} %pad_clamp_fusion.1), kind=kCustom, calls=%fused_computation.2 | custom fusion | bytes 12585984 | tf_op jit(solution)/shard_map/jit(_take)/gather | solution.py:65
  85.4 6.8 copy.116
  92.3 3.5 select_bitcast_fusion
  95.8 6.3 all-to-all-start.1
  102.5 0.8 dynamic-slice_reduce_fusion
  103.5 0.9 gather_fusion.2
  104.4 0.9 gather_fusion.3
  105.4 1.1 copy.141
  106.5 71.5 %all-to-all-done.1 = bf16[32,128,6,128]{3,0,2,1:T(8,128)(2,1)} async-done(((bf16[32,128,6,128]{3,0,2,1:T(8,128)(2,1)}), bf16[32,128,6,128]{3,0,2,1:T(8,128)(2,1)}, u32[]{:S(2)}, u32[]{:S(2)}) %all-to-all-start.1) | async-done | bytes 6291488 | tf_op jit(solution)/shard_map/all_to_all | solution.py:66
  178.0 9.5 %copy.118 = bf16[32,16,8,6,128]{4,2,3,1,0:T(8,128)(2,1)} copy(bf16[32,16,8,6,128]{4,0,3,2,1:T(8,128)(2,1)} %bitcast.8) | data formatting | bytes 12582912 | tf_op jit(solution)/shard_map/reshape | solution.py:67
  187.4 6.6 gather_fusion.1
  194.1 3.3 convert_bitcast_fusion
  197.3 13.6 %copy.119 = f32[8,32,64,128]{3,2,1,0:T(8,128)S(1)} copy(f32[8,32,64,128]{3,0,1,2:T(8,128)S(1)} %convert_bitcast_fusion) | data formatting | bytes 16777216 | tf_op jit(solution)/shard_map/convert_element_type | solution.py:85
  210.9 1.2 multiply_convert_fusion
  212.1 5.8 fusion.15
  217.9 2.3 fusion.1
  220.2 1.9 copy.127
  222.1 0.9 fusion.39
  223.1 2.7 fusion.45
  225.8 1.3 fusion.13
  227.2 1.7 fusion.20
  228.8 2.9 copy.129
  231.7 2.2 fusion.12
  233.9 1.3 copy-done.5
  235.3 93.8 %custom-call.17 = f32[8,128,128]{2,1,0:T(8,128)S(1)} custom-call(f32[8,128,128]{2,1,0:T(8,128)S(1)} %cholesky.122), custom_call_target="Cholesky" | custom-call | tf_op jit(solution)/shard_map/jit(cholesky)/cholesky | solution.py:23
  329.1 0.2 cholesky.117
  329.3 79.2 %custom-call.18 = f32[8,1,128,128]{2,3,1,0:T(8,128)} custom-call(f32[8,1,128,128]{3,2,1,0:T(8,128)S(1)} %select_bitcast_fusion.1), custom_call_target="InvertDiagBlocksLowerTriangular" | custom-call | tf_op jit(solution)/shard_map/jit(cholesky)/cholesky | solution.py:23
  408.5 1.8 constant_dynamic-update-slice_fusion.1
  410.4 3.1 convolution_subtract_fusion.1
  413.4 94.8 %custom-call.19 = f32[8,128,128]{2,1,0:T(8,128)S(1)} custom-call(f32[8,128,128]{2,1,0:T(8,128)} %convolution_subtract_fusion.1), custom_call_target="Cholesky" | custom-call | tf_op jit(solution)/shard_map/jit(cholesky)/cholesky | solution.py:23
  508.5 1.2 copy-done.4
  509.7 1.9 select_select_fusion
  511.7 5.8 while.1
  511.7 0.6 fusion.66
  512.3 2.3 bitcast_dynamic-update-slice_fusion.2
  514.6 0.6 fusion.66
  515.2 2.2 bitcast_dynamic-update-slice_fusion.2
  517.4 158.6 %custom-call.20 = f32[8,2,128,128]{2,3,1,0:T(8,128)} custom-call(f32[8,2,128,128]{3,2,1,0:T(8,128)} %bitcast.159), custom_call_target="InvertDiagBlocksLowerTriangular" | custom-call | tf_op jit(solution)/shard_map/jit(_solve_triangular)/vmap()/triangular_solve | solution.py:24
  676.1 3.1 fusion.29
  679.1 2.6 copy.135
  681.7 2.4 convolution_subtract_fusion
  684.1 2.0 fusion.28
  686.1 1.2 fusion.26
  687.3 1.8 fusion.25
  689.2 1.7 subtract_convert_fusion
  690.9 0.8 convolution_bitcast_fusion
  691.7 0.2 fusion.5
  692.0 0.6 copy.143
  692.5 18.8 %all_to_all.67 = bf16[256,8,256]{2,1,0:T(8,128)(2,1)S(1)} all-to-all(bf16[256,8,256]{2,1,0:T(8,128)(2,1)S(1)} %copy.143), channel_id=1, replica_groups=mesh['space'=16,'mem'=8] {'mem'}, dimensions={0} | all-to-all | bytes 2097152 | tf_op jit(solution)/shard_map/all_to_all | solution.py:101
  711.4 1.1 copy.196
  (74 shorter events, 2.2 us)
Async XLA Ops:
  0.0 56.3 %copy-start = (bf16[32,64,128]{2,1,0:T(8,128)(2,1)S(1)}, bf16[32,64,128]{2,1,0:T(8,128)(2,1)}, u32[]{:S(2)}) copy-start(bf16[32,64,128]{2,1,0:T(8,128)(2,1)} %param.11) | copy-start | bytes 1572868
  0.0 28.4 %copy-start.3 = (f32[64,128]{1,0:T(8,128)S(1)}, f32[64,128]{1,0:T(8,128)}, u32[]{:S(2)}) copy-start(f32[64,128]{1,0:T(8,128)} %param.12) | copy-start | bytes 98308
  0.0 43.0 %copy-start.8 = (bf16[32,64,256]{2,1,0:T(8,128)(2,1)S(1)}, bf16[32,64,256]{2,1,0:T(8,128)(2,1)}, u32[]{:S(2)}) copy-start(bf16[32,64,256]{2,1,0:T(8,128)(2,1)} %param.10) | copy-start | bytes 3145732
  5.8 20.9 %all-to-all-start = ((s32[128,1,6]{2,1,0:T(1,128)}), s32[128,1,6]{2,1,0:T(1,128)S(1)}, u32[]{:S(2)}, u32[]{:S(2)}) async-start(s32[128,1,6]{2,1,0:T(1,128)} %bitcast.3), calls=%async_computation | async-start | bytes 131072 | tf_op jit(solution)/shard_map/all_to_all | solution.py:64
  39.6 10.0 %all-to-all-start.3 = ((f32[16,6,128]{2,1,0:T(8,128)}), f32[16,6,128]{2,1,0:T(8,128)S(1)}, u32[]{:S(2)}, u32[]{:S(2)}) async-start(f32[16,6,128]{2,1,0:T(8,128)} %get-tuple-element.40), calls=%async_computation.3 | async-start | bytes 131072 | tf_op jit(solution)/shard_map/all_to_all | solution.py:76
  49.5 46.3 %all-to-all-start.4 = ((bf16[32,64,256]{2,0,1:T(8,128)(2,1)}), bf16[32,64,256]{2,0,1:T(8,128)(2,1)S(1)}, u32[]{:S(2)}, u32[]{:S(2)}) async-start(bf16[32,64,256]{2,0,1:T(8,128)(2,1)} %copy.140), calls=%async_computation.4 | async-start | bytes 2097152 | tf_op jit(solution)/shard_map/all_to_all | solution.py:96
  95.8 6.4 copy-start.10
  95.8 6.4 copy-start.9
  95.8 82.1 %all-to-all-start.1 = ((bf16[32,128,6,128]{3,0,2,1:T(8,128)(2,1)}), bf16[32,128,6,128]{3,0,2,1:T(8,128)(2,1)}, u32[]{:S(2)}, u32[]{:S(2)}) async-start(bf16[32,128,6,128]{3,0,2,1:T(8,128)(2,1)} %select_bitcast_fusion), calls=%async_computation.1 | async-start | bytes 12582912 | tf_op jit(solution)/shard_map/all_to_all | solution.py:66
  233.9 1.3 copy-start.5
  508.3 1.3 copy-start.4
  681.7 2.4 copy-start.7
  681.7 4.4 copy-start.2
  689.1 1.7 copy-start.6
  691.9 20.5 %copy-start.1 = (bf16[32,64,128]{2,1,0:T(8,128)(2,1)S(1)}, bf16[32,64,128]{2,1,0:T(8,128)(2,1)}, u32[]{:S(2)}) copy-start(bf16[32,64,128]{2,1,0:T(8,128)(2,1)} %param.11) | copy-start | bytes 1572868
where the time goes:
time: 722 us; the launch traced here: 713 us
  other arithmetic  446 us (62%)
  local copies, waits for them, and re-layouts  95.8 us (13%)
  waiting for transfers between devices  85.8 us (12%)
  blocking collectives  28.5 us (4%)
  matrix products  28.4 us (4%)
  starting transfers between devices  28 us (4%)
    another operation x9, other arithmetic, transform(): factor = jnp.linalg.cholesky(system)  268 us
    another operation x4, other arithmetic, transform(): jax.scipy.linalg.solve_triangular(factor, jnp.broadcast_to(identity, syst...  161 us
    all_to_all x1, waiting for transfers between devices, body(): lax.all_to_all(outgoing, ('space', 'mem'), split_axis=1, concat_axis=1, t...  71.5 us
    gather x2, local copies, waits for them, and re-layouts, body(): outgoing = jnp.take(obs_ens, asked_ids, axis=1)  35.9 us
    all_to_all x1, blocking collectives, body(): lax.all_to_all(updated, 'mem', split_axis=0, concat_axis=1, tiled=True)  18.8 us
  transfers between devices with their start and end apart: 4, of which 3 were waited for; matrix products, arithmetic and copies ran while one was open for 6% of the time, Pallas kernels for 0%

commit v1 on v0

--- a/solution.py
+++ b/solution.py
@@ -98,7 +98,10 @@
         "krp,rkj->jrp", region_states, mix_parts, preferred_element_type=jnp.float32
     )
     updated = (both_parts[:members] + both_parts[members:]).astype(jnp.bfloat16)
-    return lax.all_to_all(updated, "mem", split_axis=0, concat_axis=1, tiled=True)
+    return jnp.concatenate(
+        lax.all_to_all(jnp.stack(jnp.split(updated, lax.axis_size("mem"), axis=0)), "mem", 0, 0),
+        axis=1,
+    )
 
 
 def solution(mesh):

time: 722 us -> 721 us (level)
    another operation x9 -> x10, other arithmetic: 268 us -> 268 us  [transform(): factor = jnp.linalg.cholesky(system)]
where the time goes in v1:
time: 721 us; the launch traced here: 712 us
  other arithmetic  446 us (62%)
  local copies, waits for them, and re-layouts  94.9 us (13%)
  waiting for transfers between devices  85.8 us (12%)
  blocking collectives  28.7 us (4%)
  matrix products  28.4 us (4%)
  starting transfers between devices  28 us (4%)
    another operation x10, other arithmetic, transform(): factor = jnp.linalg.cholesky(system)  268 us
    another operation x4, other arithmetic, transform(): jax.scipy.linalg.solve_triangular(factor, jnp.broadcast_to(identity, syst...  161 us
    all_to_all x1, waiting for transfers between devices, body(): lax.all_to_all(outgoing, ('space', 'mem'), split_axis=1, concat_axis=1, t...  71.5 us
    gather x2, local copies, waits for them, and re-layouts, body(): outgoing = jnp.take(obs_ens, asked_ids, axis=1)  36 us
    all_to_all x1, blocking collectives, body(): lax.all_to_all(jnp.stack(jnp.split(updated, lax.axis_size('mem'), axis=0)...  19 us
  transfers between devices with their start and end apart: 4, of which 3 were waited for; matrix products, arithmetic and copies ran while one was open for 6% of the time, Pallas kernels for 0%

profile of v1, /device:TPU:1, one launch (start us, length us, event | category | flops | bytes accessed | tf_op | source)
XLA Modules:
  0.0 712.4 jit_solution(5923969030909888357)
XLA Ops:
  0.0 0.9 constant_dynamic-slice_fusion.2
  1.3 0.2 select_reduce_fusion.2
  1.6 3.5 scatter_fusion
  5.1 0.6 broadcast_in_dim.30.clone
  5.8 11.5 %all-to-all-start = ((s32[128,1,6]{2,1,0:T(1,128)}), s32[128,1,6]{2,1,0:T(1,128)S(1)}, u32[]{:S(2)}, u32[]{:S(2)}) async-start(s32[128,1,6]{2,1,0:T(1,128)} %bitcast.3), calls=%async_computation | async-start | bytes 131072 | tf_op jit(solution)/shard_map/all_to_all | solution.py:64
  17.3 9.4 %all-to-all-done = s32[128,1,6]{2,1,0:T(1,128)S(1)} async-done(((s32[128,1,6]{2,1,0:T(1,128)}), s32[128,1,6]{2,1,0:T(1,128)S(1)}, u32[]{:S(2)}, u32[]{:S(2)}) %all-to-all-start) | async-done | bytes 3104 | tf_op jit(solution)/shard_map/all_to_all | solution.py:64
  27.0 0.1 reshape.292
  27.2 0.6 gather_fusion.4
  27.8 0.6 gather_fusion.5
  28.5 0.7 broadcast_select_fusion.1
  29.3 9.7 %all_to_all.53 = f32[16,6,128]{2,1,0:T(8,128)S(1)} all-to-all(f32[16,6,128]{2,1,0:T(8,128)S(1)} %get-tuple-element.39), channel_id=1, replica_groups=mesh['space'=16,'mem'=8] {'space'}, dimensions={0} | all-to-all | bytes 98304 | tf_op jit(solution)/shard_map/all_to_all | solution.py:75
  39.0 3.5 all-to-all-start.3
  42.5 1.6 copy.139
  44.0 4.9 all-to-all-done.3
  48.9 6.6 all-to-all-start.4
  55.6 29.2 %gather_fusion = bf16[768,32,128]{2,0,1:T(8,128)(2,1)} fusion(bf16[32,64,128]{2,1,0:T(8,128)(2,1)S(1)} %copy-done, s32[1024]{0:T(1024)S(1)} %get-tuple-element.46), kind=kCustom, calls=%fused_computation.2 | custom fusion | bytes 12585984 | tf_op jit(solution)/shard_map/jit(_take)/gather | solution.py:65
  84.8 6.8 copy.115
  91.6 3.5 select_bitcast_fusion
  95.2 6.3 all-to-all-start.1
  101.9 0.8 dynamic-slice_reduce_fusion
  102.9 0.9 gather_fusion.2
  103.8 0.9 gather_fusion.3
  104.8 1.1 copy.140
  105.8 71.5 %all-to-all-done.1 = bf16[32,128,6,128]{3,0,2,1:T(8,128)(2,1)} async-done(((bf16[32,128,6,128]{3,0,2,1:T(8,128)(2,1)}), bf16[32,128,6,128]{3,0,2,1:T(8,128)(2,1)}, u32[]{:S(2)}, u32[]{:S(2)}) %all-to-all-start.1) | async-done | bytes 6291488 | tf_op jit(solution)/shard_map/all_to_all | solution.py:66
  177.3 9.5 %copy.117 = bf16[32,16,8,6,128]{4,2,3,1,0:T(8,128)(2,1)} copy(bf16[32,16,8,6,128]{4,0,3,2,1:T(8,128)(2,1)} %bitcast.8) | data formatting | bytes 12582912 | tf_op jit(solution)/shard_map/reshape | solution.py:67
  186.8 6.6 gather_fusion.1
  193.4 3.3 convert_bitcast_fusion
  196.7 13.6 %copy.118 = f32[8,32,64,128]{3,2,1,0:T(8,128)S(1)} copy(f32[8,32,64,128]{3,0,1,2:T(8,128)S(1)} %convert_bitcast_fusion) | data formatting | bytes 16777216 | tf_op jit(solution)/shard_map/convert_element_type | solution.py:85
  210.2 1.2 multiply_convert_fusion
  211.4 5.8 fusion.15
  217.3 2.3 fusion.1
  219.6 1.9 copy.126
  221.5 0.9 fusion.47
  222.4 2.7 fusion.53
  225.2 1.3 fusion.13
  226.5 1.7 fusion.20
  228.2 2.9 copy.128
  231.1 2.2 fusion.12
  233.3 1.3 copy-done.6
  234.6 93.8 %custom-call.17 = f32[8,128,128]{2,1,0:T(8,128)S(1)} custom-call(f32[8,128,128]{2,1,0:T(8,128)S(1)} %cholesky.122), custom_call_target="Cholesky" | custom-call | tf_op jit(solution)/shard_map/jit(cholesky)/cholesky | solution.py:23
  328.4 0.2 cholesky.117
  328.7 79.2 %custom-call.18 = f32[8,1,128,128]{2,3,1,0:T(8,128)} custom-call(f32[8,1,128,128]{3,2,1,0:T(8,128)S(1)} %select_bitcast_fusion.1), custom_call_target="InvertDiagBlocksLowerTriangular" | custom-call | tf_op jit(solution)/shard_map/jit(cholesky)/cholesky | solution.py:23
  407.9 1.8 constant_dynamic-update-slice_fusion.1
  409.7 3.1 convolution_subtract_fusion.1
  412.8 94.8 %custom-call.19 = f32[8,128,128]{2,1,0:T(8,128)S(1)} custom-call(f32[8,128,128]{2,1,0:T(8,128)} %convolution_subtract_fusion.1), custom_call_target="Cholesky" | custom-call | tf_op jit(solution)/shard_map/jit(cholesky)/cholesky | solution.py:23
  508.0 1.1 copy-done.5
  509.0 1.9 select_select_fusion
  511.0 5.7 while.1
  511.1 0.6 fusion.74
  511.6 2.3 bitcast_dynamic-update-slice_fusion.2
  513.9 0.6 fusion.74
  514.5 2.2 bitcast_dynamic-update-slice_fusion.2
  516.7 158.6 %custom-call.20 = f32[8,2,128,128]{2,3,1,0:T(8,128)} custom-call(f32[8,2,128,128]{3,2,1,0:T(8,128)} %bitcast.188), custom_call_target="InvertDiagBlocksLowerTriangular" | custom-call | tf_op jit(solution)/shard_map/jit(_solve_triangular)/vmap()/triangular_solve | solution.py:24
  675.4 3.1 fusion.29
  678.5 2.6 copy.134
  681.0 2.4 convolution_subtract_fusion
  683.4 2.0 fusion.28
  685.4 1.2 fusion.26
  686.6 1.8 fusion.25
  688.5 1.7 subtract_convert_fusion
  690.2 0.8 convolution_bitcast_fusion
  691.0 0.2 fusion.5
  691.4 19.0 %all_to_all.54 = bf16[8,32,8,256]{3,1,2,0:T(8,128)(2,1)S(1)} all-to-all(bf16[8,32,8,256]{3,1,2,0:T(8,128)(2,1)S(1)} %fusion.37), channel_id=1, replica_groups=mesh['space'=16,'mem'=8] {'mem'}, dimensions={0} | all-to-all | bytes 2097152 | tf_op jit(solution)/shard_map/all_to_all | solution.py:102
  710.4 1.6 copy.142
  (83 shorter events, 2.3 us)
Async XLA Ops:
  0.0 55.6 %copy-start = (bf16[32,64,128]{2,1,0:T(8,128)(2,1)S(1)}, bf16[32,64,128]{2,1,0:T(8,128)(2,1)}, u32[]{:S(2)}) copy-start(bf16[32,64,128]{2,1,0:T(8,128)(2,1)} %param.11) | copy-start | bytes 1572868
  0.0 27.2 %copy-start.3 = (f32[64,128]{1,0:T(8,128)S(1)}, f32[64,128]{1,0:T(8,128)}, u32[]{:S(2)}) copy-start(f32[64,128]{1,0:T(8,128)} %param.13) | copy-start | bytes 98308
  0.0 27.8 %copy-start.4 = (f32[64,128]{1,0:T(8,128)S(1)}, f32[64,128]{1,0:T(8,128)}, u32[]{:S(2)}) copy-start(f32[64,128]{1,0:T(8,128)} %param.12) | copy-start | bytes 98308
  0.0 42.5 %copy-start.9 = (bf16[32,64,256]{2,1,0:T(8,128)(2,1)S(1)}, bf16[32,64,256]{2,1,0:T(8,128)(2,1)}, u32[]{:S(2)}) copy-start(bf16[32,64,256]{2,1,0:T(8,128)(2,1)} %param.10) | copy-start | bytes 3145732
  5.8 20.9 %all-to-all-start = ((s32[128,1,6]{2,1,0:T(1,128)}), s32[128,1,6]{2,1,0:T(1,128)S(1)}, u32[]{:S(2)}, u32[]{:S(2)}) async-start(s32[128,1,6]{2,1,0:T(1,128)} %bitcast.3), calls=%async_computation | async-start | bytes 131072 | tf_op jit(solution)/shard_map/all_to_all | solution.py:64
  39.0 10.0 %all-to-all-start.3 = ((f32[16,6,128]{2,1,0:T(8,128)}), f32[16,6,128]{2,1,0:T(8,128)S(1)}, u32[]{:S(2)}, u32[]{:S(2)}) async-start(f32[16,6,128]{2,1,0:T(8,128)} %get-tuple-element.40), calls=%async_computation.3 | async-start | bytes 131072 | tf_op jit(solution)/shard_map/all_to_all | solution.py:76
  48.9 46.2 %all-to-all-start.4 = ((bf16[32,64,256]{2,0,1:T(8,128)(2,1)}), bf16[32,64,256]{2,0,1:T(8,128)(2,1)S(1)}, u32[]{:S(2)}, u32[]{:S(2)}) async-start(bf16[32,64,256]{2,0,1:T(8,128)(2,1)} %copy.139), calls=%async_computation.4 | async-start | bytes 2097152 | tf_op jit(solution)/shard_map/all_to_all | solution.py:96
  95.2 6.4 copy-start.11
  95.2 6.4 copy-start.10
  95.2 82.1 %all-to-all-start.1 = ((bf16[32,128,6,128]{3,0,2,1:T(8,128)(2,1)}), bf16[32,128,6,128]{3,0,2,1:T(8,128)(2,1)}, u32[]{:S(2)}, u32[]{:S(2)}) async-start(bf16[32,128,6,128]{3,0,2,1:T(8,128)(2,1)} %select_bitcast_fusion), calls=%async_computation.1 | async-start | bytes 12582912 | tf_op jit(solution)/shard_map/all_to_all | solution.py:66
  233.3 1.3 copy-start.6
  507.7 1.3 copy-start.5
  681.0 2.4 copy-start.8
  681.0 4.4 copy-start.2
  688.5 1.7 copy-start.7
  691.4 20.5 %copy-start.1 = (bf16[32,64,128]{2,1,0:T(8,128)(2,1)S(1)}, bf16[32,64,128]{2,1,0:T(8,128)(2,1)}, u32[]{:S(2)}) copy-start(bf16[32,64,128]{2,1,0:T(8,128)(2,1)} %param.11) | copy-start | bytes 1572868
